TPU v7x, 32 devices: a whole 2x2x4 slice. The times are simulated.
32 devices in a mesh: dp: 8 (over z, y), expert: 4 (over x, core).
Axes of the slice: x: 2, y: 2, z: 4, core: 2. Of those that a mesh axis runs over, the one named last changes fastest.
Arguments:
- tokens: bfloat16 [1024, 4096], P('dp'), may hold values from -6 to 6
- upstream: bfloat16 [1024, 4096], P('dp', 'expert'), may hold values from -6 to 6
- gates: bfloat16 [1024, 2], P('dp'), may hold values from 0.049804688 to 1
- expert_ids: int32 [1024, 2], P('dp'), may hold values from 0 to 7, all different within a row; in each aligned block of 128 rows (0 to 127, 128 to 255, ...) at most 64 rows name the same one
- w_gate: bfloat16 [8, 1536, 4096], P('dp', 'expert'), may hold values from -0.09375 to 0.09375
- w_up: bfloat16 [8, 1536, 4096], P('dp', 'expert'), may hold values from -0.09375 to 0.09375
- w_down: bfloat16 [8, 1536, 4096], P('dp', 'expert'), may hold values from -0.15625 to 0.15625
Outputs:
- grad_x: bfloat16 [1024, 4096], P('dp', 'expert')
- grad_gates: float32 [1024, 2], P('dp')
- grad_w_gate: bfloat16 [8, 1536, 4096], P('dp', 'expert')
- grad_w_up: bfloat16 [8, 1536, 4096], P('dp', 'expert')
- grad_w_down: bfloat16 [8, 1536, 4096], P('dp', 'expert')
Inputs may be any that keep to these rules, and one draw needn't show every extreme that they name: `expert_ids`: each row names 2 different experts. In each aligned block of 128 rows (the tokens of one index of dp) no expert is named by more than 64 rows, a bound that some block reaches.
All inputs are finite; a program needn't handle non-finite values.
Results may differ from a plain program's by a relative error of at most 0.012.
Values may be sent and summed in bfloat16 or wider, within the bound.
A program may use at most 128 MiB of HBM per device.

v0:
```python
import jax
import jax.numpy as jnp
from jax import lax
from jax.sharding import PartitionSpec as P


def swish_pair(pre):
    sigma = jax.nn.sigmoid(pre)
    return (pre * sigma, sigma * (1.0 + pre * (1.0 - sigma)))


def contract_last(left, right):
    return lax.dot_general(
        left, right, (((1,), (1,)), ((), ())), preferred_element_type=jnp.float32
    )


def contract_first(left, right):
    return lax.dot_general(
        left, right, (((0,), (0,)), ((), ())), preferred_element_type=jnp.float32
    )


def expert_backward(inputs, upward, scale_col, w_g, w_u, w_d):
    pre_gate = contract_last(inputs, w_g)
    pre_up = contract_last(inputs, w_u)
    swish, slope = swish_pair(pre_gate)
    act = (swish * pre_up).astype(jnp.bfloat16)
    act_f = act.astype(jnp.float32)
    back = contract_last(upward, w_d)
    gate_term = jnp.sum(act_f * back, axis=1)
    scaled = (scale_col * act_f).astype(jnp.bfloat16)
    grad_down = contract_first(scaled, upward).astype(jnp.bfloat16)
    weighted = scale_col * back
    d_gate = (weighted * pre_up * slope).astype(jnp.bfloat16)
    d_up = (weighted * swish).astype(jnp.bfloat16)
    grad_gate = contract_first(d_gate, inputs).astype(jnp.bfloat16)
    grad_up = contract_first(d_up, inputs).astype(jnp.bfloat16)
    piece = jnp.dot(d_gate, w_g, preferred_element_type=jnp.float32)
    piece = piece + jnp.dot(d_up, w_u, preferred_element_type=jnp.float32)
    return (piece.astype(jnp.bfloat16), gate_term, grad_gate, grad_up, grad_down)


def per_device(tokens, upstream, gates, expert_ids, w_gate, w_up, w_down):
    groups = lax.axis_size("dp")
    experts = groups * w_gate.shape[0]
    tok_rows, width = tokens.shape
    top = expert_ids.shape[1]
    cap = 2 * tok_rows * top // experts
    part = upstream.shape[1]
    rows = experts * cap
    own = lax.axis_index("expert")
    tok_part = lax.dynamic_slice_in_dim(tokens, own * part, part, axis=1)
    flat = expert_ids.reshape(-1)
    count = flat.shape[0]
    earlier = jnp.arange(count)[None, :] < jnp.arange(count)[:, None]
    same = flat[:, None] == flat[None, :]
    position = jnp.sum((earlier & same).astype(jnp.int32), axis=1)
    slot = (flat * cap + position).reshape(tok_rows, top)
    hit = slot[None, :, :] == jnp.arange(rows, dtype=jnp.int32)[:, None, None]
    pick = jnp.sum(hit.astype(jnp.float32), axis=2).astype(jnp.bfloat16)
    scale = jnp.sum(jnp.where(hit, gates.astype(jnp.float32)[None], 0.0), axis=(1, 2))
    packed = jnp.concatenate([tok_part, upstream], axis=1)
    send = jnp.dot(pick, packed, preferred_element_type=jnp.float32).astype(jnp.bfloat16)
    send = jnp.concatenate(
        [send, jnp.broadcast_to(scale[:, None], (rows, 128)).astype(jnp.bfloat16)], axis=1
    )
    got = lax.all_to_all(send, "dp", split_axis=0, concat_axis=0, tiled=True)
    inputs = lax.all_gather(got[:, :part], "expert", axis=1, tiled=True)
    upward = lax.all_gather(got[:, part : 2 * part], "expert", axis=1, tiled=True)
    scale_col = got[:, 2 * part : 2 * part + 1].astype(jnp.float32)
    piece, term, grad_gate, grad_up, grad_down = expert_backward(
        inputs, upward, scale_col, w_gate[0], w_up[0], w_down[0]
    )
    total = lax.psum(term, "expert")
    summed = lax.psum_scatter(piece, "expert", scatter_dimension=1, tiled=True)
    high = total.astype(jnp.bfloat16)
    low = (total - high.astype(jnp.float32)).astype(jnp.bfloat16)
    lane = lax.broadcasted_iota(jnp.int32, (rows, 128), 1)
    tail = jnp.where(lane == 0, high[:, None], low[:, None])
    home = lax.all_to_all(
        jnp.concatenate([summed, tail], axis=1), "dp", split_axis=0, concat_axis=0, tiled=True
    )
    grad_x = contract_first(pick, home[:, :part]).astype(jnp.bfloat16)
    terms = home[:, part].astype(jnp.float32) + home[:, part + 1].astype(jnp.float32)
    grad_gates = jnp.sum(jnp.where(hit, terms[:, None, None], 0.0), axis=0)
    return (grad_x, grad_gates, grad_gate[None], grad_up[None], grad_down[None])


def solution(mesh):
    in_specs = (
        P("dp", None),
        P("dp", "expert"),
        P("dp", None),
        P("dp", None),
        P("dp", "expert", None),
        P("dp", "expert", None),
        P("dp", "expert", None),
    )
    out_specs = (
        P("dp", "expert"),
        P("dp", None),
        P("dp", "expert", None),
        P("dp", "expert", None),
        P("dp", "expert", None),
    )
    return jax.shard_map(
        per_device, mesh=mesh, in_specs=in_specs, out_specs=out_specs, check_vma=False
    )
```

profile of v0, /device:TPU:0, one launch (start us, length us, event | category | flops | bytes accessed | tf_op | source)
XLA Modules:
  0.0 249.7 jit_solution(17244349848035692851)
XLA Ops:
  7.2 0.0 copy-start
  7.2 0.0 all-gather.5.cloned.1.call-start
  7.2 0.9 copy.28
  8.2 0.1 eq.35
  8.3 0.2 convert_reduce_fusion.2
  8.5 0.1 reduce_sum.48
  8.6 0.1 copy.29
  8.7 0.7 multiply_add_fusion
  9.4 0.7 convert_element_type.79
  10.1 1.0 constant_dynamic-slice_fusion
  11.0 0.2 convert_reduce_fusion
  11.2 1.6 convolution_convert_fusion.3
  12.9 0.1 broadcast_in_dim.62
  13.0 0.2 pad_maximum_fusion
  13.2 58.5 %all_to_all.24 = bf16[8,64,2176]{2,1,0:T(8,128)(2,1)S(1)} all-to-all(bf16[8,64,2176]{2,1,0:T(8,128)(2,1)S(1)} %bitcast.39), channel_id=1, replica_groups=mesh['dp'=8,'expert'=4] {'dp'}, dimensions={0} | all-to-all | bytes 4456448 | tf_op jit(solution)/shard_map/all_to_all | solution.py:68
  71.7 0.0 copy-start.1
  71.7 1.4 copy-done.1
  73.0 1.6 fusion.25
  74.6 0.0 all-gather.5.cloned.1.call-update
  74.7 0.0 all-gather.3.cloned.1.call-start
  74.7 0.7 all-gather.3.cloned.1.call-update
  75.4 0.0 reduce-scatter.2.cloned.1.call-start
  75.5 1.0 convert_reduce_fusion.1
  76.5 31.5 %all-gather.5.cloned.1.call-done = bf16[512,4096]{1,0:T(8,128)(2,1)} async-done(((bf16[512,1024]{1,0:T(8,128)(2,1)}), bf16[512,4096]{1,0:T(8,128)(2,1)}) %all-gather.5.cloned.1.call-update) | async-done | bytes 4194320 | tf_op jit(solution)/shard_map/all_gather | solution.py:69
  108.0 0.0 copy-done
  108.0 0.0 copy-start.2
  108.0 0.0 copy-start.7
  108.0 5.0 %fusion.5 = f32[512,384]{0,1:T(8,128)} fusion(bf16[512,4096]{1,0:T(8,128)(2,1)} %all-gather.5.cloned.1.call-done, bf16[1,384,4096]{2,1,0:T(8,128)(2,1)S(1)} %copy-done), kind=kOutput, calls=%fused_computation.9 | convolution fusion | flops 1610612736 | bytes 8126464 | tf_op jit(solution)/shard_map/dot_general | solution.py:13
  113.0 0.0 copy-done.2
  113.0 0.0 copy-done.7
  113.0 2.7 %fusion.8 = f32[512,384]{0,1:T(8,128)} fusion(bf16[512,4096]{1,0:T(8,128)(2,1)S(1)} %copy-done.7, bf16[1,384,4096]{2,1,0:T(8,128)(2,1)S(1)} %copy-done.2), kind=kOutput, calls=%fused_computation.12 | convolution fusion | flops 1610612736 | bytes 8126464 | tf_op jit(solution)/shard_map/dot_general | solution.py:13
  115.7 28.9 %all-gather.3.cloned.1.call-done = bf16[512,4096]{1,0:T(8,128)(2,1)} async-done(((bf16[512,1024]{1,0:T(8,128)(2,1)}), bf16[512,4096]{1,0:T(8,128)(2,1)}) %all-gather.3.cloned.1.call-update) | async-done | bytes 4194320 | tf_op jit(solution)/shard_map/all_gather | solution.py:70
  144.6 6.4 %fusion.13 = (f32[512]{0:T(512)S(1)}, bf16[512,384]{0,1:T(8,128)(2,1)}, bf16[512,384]{0,1:T(8,128)(2,1)S(1)}, bf16[512,384]{0,1:T(8,128)(2,1)S(1)}) fusion(f32[512,384]{0,1:T(8,128)} %fusion.8, f32[512,384]{0,1:T(8,128)} %fusion.5, f32[512]{0:T(512)S(1)} %convert_reduce_fusion.1, bf16[512,4096]{1,0:T(8,128)(2,1)} %all-gather.3.cloned.1.call-done, ...), kind=kOutput, calls=%fused_computation.23 | convolution fusion | flops 1614347776 | bytes 10096640 | tf_op jit(solution)/shard_map/dot_general | solution.py:13
  151.0 0.0 copy-start.6
  151.0 0.0 copy-start.4
  151.0 0.0 copy-start.3
  151.0 2.4 fusion.3
  153.4 0.0 copy-done.6
  153.4 0.0 copy-done.4
  153.4 0.0 copy-done.3
  153.4 4.6 %add_convert_fusion = bf16[512,4096]{1,0:T(8,128)(2,1)} fusion(f32[512,4096]{1,0:T(8,128)S(1)} %fusion.3, bf16[512,384]{0,1:T(8,128)(2,1)S(1)} %get-tuple-element.14, bf16[1,384,4096]{2,1,0:T(8,128)(2,1)S(1)} %copy-done.3), kind=kOutput, calls=%fused_computation | convolution fusion | flops 1614807040 | bytes 16121856 | tf_op jit(solution)/shard_map/dot_general | solution.py:40
  158.0 0.0 reduce-scatter.2.cloned.1.call-update
  158.0 5.9 %psum.7 = f32[512]{0:T(512)S(1)} all-reduce(f32[512]{0:T(512)S(1)} %get-tuple-element.9), channel_id=1, replica_groups=mesh['dp'=8,'expert'=4] {'expert'}, use_global_device_ids=true, to_apply=%region_5.6 | all-reduce | flops 512 | bytes 4096 | tf_op jit(solution)/shard_map/psum | solution.py:75
  163.9 0.2 broadcast_select_fusion
  164.1 38.5 %reduce-scatter.2.cloned.1.call-done = bf16[512,1024]{1,0:T(8,128)(2,1)} async-done(((bf16[512,4096]{1,0:T(8,128)(2,1)}), bf16[512,1024]{1,0:T(8,128)(2,1)}) %reduce-scatter.2.cloned.1.call-update) | async-done | bytes 1048592 | tf_op jit(solution)/shard_map/reduce_scatter | solution.py:76
  202.6 2.4 pad_maximum_fusion.1
  205.0 5.5 %all-to-all-start.1 = ((bf16[8,64,1152]{2,1,0:T(8,128)(2,1)}), bf16[8,64,1152]{2,1,0:T(8,128)(2,1)}, u32[]{:S(2)}, u32[]{:S(2)}) async-start(bf16[8,64,1152]{2,1,0:T(8,128)(2,1)} %bitcast.40), calls=%async_computation.2 | async-start | bytes 2359296 | tf_op jit(solution)/shard_map/all_to_all | solution.py:81
  210.5 0.0 copy-start.5
  210.5 0.0 copy-start.8
  210.5 5.9 %fusion = bf16[1,384,4096]{2,1,0:T(8,128)(2,1)} fusion(bf16[512,384]{0,1:T(8,128)(2,1)} %copy-done.6, bf16[512,4096]{1,0:T(8,128)(2,1)} %all-gather.5.cloned.1.call-done), kind=kOutput, calls=%fused_computation.4 | convolution fusion | flops 1612185600 | bytes 7733248 | tf_op jit(solution)/shard_map/dot_general | solution.py:19
  216.4 0.0 copy-done.5
  216.4 0.0 copy-done.8
  216.4 0.0 copy-start.9
  216.4 0.0 copy-start.10
  216.5 3.5 %fusion.1 = bf16[1,384,4096]{2,1,0:T(8,128)(2,1)} fusion(bf16[512,384]{0,1:T(8,128)(2,1)S(1)} %copy-done.5, bf16[512,4096]{1,0:T(8,128)(2,1)S(1)} %copy-done.8), kind=kOutput, calls=%fused_computation.5 | convolution fusion | flops 1612185600 | bytes 7733248 | tf_op jit(solution)/shard_map/dot_general | solution.py:19
  219.9 0.0 copy-done.9
  219.9 0.0 copy-done.10
  219.9 3.5 %fusion.2 = bf16[1,384,4096]{2,1,0:T(8,128)(2,1)} fusion(bf16[512,4096]{1,0:T(8,128)(2,1)S(1)} %copy-done.9, bf16[512,384]{0,1:T(8,128)(2,1)S(1)} %copy-done.10, f32[512]{0:T(512)S(1)} %convert_reduce_fusion.1), kind=kOutput, calls=%fused_computation.6 | convolution fusion | flops 1612775424 | bytes 7735296 | tf_op jit(solution)/shard_map/dot_general | solution.py:19
  223.4 15.6 %all-to-all-done.1 = bf16[8,64,1152]{2,1,0:T(8,128)(2,1)} async-done(((bf16[8,64,1152]{2,1,0:T(8,128)(2,1)}), bf16[8,64,1152]{2,1,0:T(8,128)(2,1)}, u32[]{:S(2)}, u32[]{:S(2)}) %all-to-all-start.1) | async-done | bytes 1179680 | tf_op jit(solution)/shard_map/all_to_all | solution.py:81
  239.0 2.3 convolution_convert_fusion.4
  241.3 1.2 add_reduce_fusion
  242.5 0.7 select_reduce_fusion
  (2 shorter events, 0.0 us)
Async XLA Ops:
  7.2 100.8 %copy-start = (bf16[1,384,4096]{2,1,0:T(8,128)(2,1)S(1)}, bf16[1,384,4096]{2,1,0:T(8,128)(2,1)}, u32[]{:S(2)}) copy-start(bf16[1,384,4096]{2,1,0:T(8,128)(2,1)} %param.11) | copy-start | bytes 9437188
  7.2 100.8 %all-gather.5.cloned.1.call-start = ((), (), s32[]{:S(2)}) async-start(), calls=%async_computation.4 | async-start | bytes 5242880 | tf_op jit(solution)/shard_map/all_gather | solution.py:69
  71.7 1.4 copy-start.1
  74.7 69.9 %all-gather.3.cloned.1.call-start = ((), (), s32[]{:S(2)}) async-start(), calls=%async_computation.3 | async-start | bytes 5242880 | tf_op jit(solution)/shard_map/all_gather | solution.py:70
  75.4 127.2 %reduce-scatter.2.cloned.1.call-start = ((), (), s32[]{:S(2)}) async-start(), calls=%async_computation.5 | async-start | bytes 5242880 | tf_op jit(solution)/shard_map/reduce_scatter | solution.py:76
  108.0 5.0 %copy-start.2 = (bf16[1,384,4096]{2,1,0:T(8,128)(2,1)S(1)}, bf16[1,384,4096]{2,1,0:T(8,128)(2,1)}, u32[]{:S(2)}) copy-start(bf16[1,384,4096]{2,1,0:T(8,128)(2,1)} %param.12) | copy-start | bytes 9437188
  108.0 5.0 %copy-start.7 = (bf16[512,4096]{1,0:T(8,128)(2,1)S(1)}, bf16[512,4096]{1,0:T(8,128)(2,1)}, u32[]{:S(2)}) copy-start(bf16[512,4096]{1,0:T(8,128)(2,1)} %all-gather.5.cloned.1.call-done) | copy-start | bytes 12582916
  151.0 2.4 copy-start.6
  151.0 2.4 copy-start.4
  151.0 2.4 copy-start.3
  205.0 34.0 %all-to-all-start.1 = ((bf16[8,64,1152]{2,1,0:T(8,128)(2,1)}), bf16[8,64,1152]{2,1,0:T(8,128)(2,1)}, u32[]{:S(2)}, u32[]{:S(2)}) async-start(bf16[8,64,1152]{2,1,0:T(8,128)(2,1)} %bitcast.40), calls=%async_computation.2 | async-start | bytes 2359296 | tf_op jit(solution)/shard_map/all_to_all | solution.py:81
  210.5 5.9 %copy-start.5 = (bf16[512,384]{0,1:T(8,128)(2,1)S(1)}, bf16[512,384]{0,1:T(8,128)(2,1)}, u32[]{:S(2)}) copy-start(bf16[512,384]{0,1:T(8,128)(2,1)} %copy-done.4) | copy-start | bytes 1179652
  210.5 5.9 %copy-start.8 = (bf16[512,4096]{1,0:T(8,128)(2,1)S(1)}, bf16[512,4096]{1,0:T(8,128)(2,1)}, u32[]{:S(2)}) copy-start(bf16[512,4096]{1,0:T(8,128)(2,1)} %all-gather.5.cloned.1.call-done) | copy-start | bytes 12582916
  216.4 3.5 %copy-start.9 = (bf16[512,4096]{1,0:T(8,128)(2,1)S(1)}, bf16[512,4096]{1,0:T(8,128)(2,1)}, u32[]{:S(2)}) copy-start(bf16[512,4096]{1,0:T(8,128)(2,1)} %all-gather.3.cloned.1.call-done) | copy-start | bytes 12582916
  216.4 3.5 %copy-start.10 = (bf16[512,384]{0,1:T(8,128)(2,1)S(1)}, bf16[512,384]{0,1:T(8,128)(2,1)}, u32[]{:S(2)}) copy-start(bf16[512,384]{0,1:T(8,128)(2,1)} %get-tuple-element.10) | copy-start | bytes 1179652
Sparse Core Ops, SparseCore 0:
  74.8 33.1 all-gather.4
  110.1 34.4 all-gather.2
  158.1 44.4 reduce-scatter.1
where the time goes:
time: 250 us
  waiting for transfers between devices  115 us (46%)
  blocking collectives  64.4 us (26%)
  matrix products  37.9 us (15%)
  between operations  13.9 us (6%)
  other arithmetic  7.47 us (3%)
  starting transfers between devices  5.61 us (2%)
  local copies, waits for them, and re-layouts  5.38 us (2%)
    all_to_all x1, blocking collectives, per_device(): got = lax.all_to_all(send, 'dp', split_axis=0, concat_axis=0, tiled=True)  58.5 us
    reduce_scatter x1, waiting for transfers between devices, per_device(): summed = lax.psum_scatter(piece, 'expert', scatter_dimension=1, tiled=True)  38.5 us
    all_gather x1, waiting for transfers between devices, per_device(): inputs = lax.all_gather(got[:, :part], 'expert', axis=1, tiled=True)  31.5 us
    all_gather x1, waiting for transfers between devices, per_device(): upward = lax.all_gather(got[:, part:2 * part], 'expert', axis=1, tiled=True)  28.9 us
    all_to_all x1, waiting for transfers between devices, per_device(): lax.all_to_all(jnp.concatenate([summed, tail], axis=1), 'dp', split_axis=...  15.6 us
    dot_general x4, matrix products, contract_first(): lax.dot_general(left, right, (((0,), (0,)), ((), ())), preferred_element_...  15.1 us
    dot_general x3, matrix products, contract_last(): lax.dot_general(left, right, (((1,), (1,)), ((), ())), preferred_element_...  14.1 us
    psum x1, blocking collectives, per_device(): total = lax.psum(term, 'expert')  5.9 us
  transfers between devices with their start and end apart: 4, of which 4 were waited for; matrix products, arithmetic and copies ran while one was open for 9% of the time, Pallas kernels for 0%

commit v1 on v0

--- a/solution.py
+++ b/solution.py
@@ -67,7 +67,9 @@
     )
     got = lax.all_to_all(send, "dp", split_axis=0, concat_axis=0, tiled=True)
     inputs = lax.all_gather(got[:, :part], "expert", axis=1, tiled=True)
-    upward = lax.all_gather(got[:, part : 2 * part], "expert", axis=1, tiled=True)
+    part_2 = got[:, part : 2 * part]
+    blocks = lax.all_gather(part_2, "expert")
+    upward = jnp.concatenate(blocks, axis=1)
     scale_col = got[:, 2 * part : 2 * part + 1].astype(jnp.float32)
     piece, term, grad_gate, grad_up, grad_down = expert_backward(
         inputs, upward, scale_col, w_gate[0], w_up[0], w_down[0]

time: 250 us -> 254 us (1.016)
  local copies, waits for them, and re-layouts: 5.38 us -> 13.2 us
  matrix products: 37.9 us -> 32.6 us
    reshape x0 -> x1, local copies, waits for them, and re-layouts: none -> 6.2 us  [per_device(): upward = jnp.concatenate(blocks, axis=1)]
    dot_general x3, matrix products: 14.1 us -> 8.84 us  [contract_last(): lax.dot_general(left, right, (((1,), (1,)), ((), ())), preferred_element_...]
    all_gather x1, waiting for transfers between devices: 28.9 us -> 31.5 us  [per_device(): blocks = lax.all_gather(part_2, 'expert')]
  transfers between devices with their start and end apart: 4 -> 4, of which waited for: 4 -> 4; matrix products, arithmetic and copies ran while one was open for 9% -> 8% of each run, Pallas kernels for 0% -> 0%
where the time goes in v1:
time: 254 us
  waiting for transfers between devices  117 us (46%)
  blocking collectives  64.4 us (25%)
  matrix products  32.6 us (13%)
  between operations  13.9 us (5%)
  local copies, waits for them, and re-layouts  13.2 us (5%)
  other arithmetic  7.49 us (3%)
  starting transfers between devices  5.63 us (2%)
    all_to_all x1, blocking collectives, per_device(): got = lax.all_to_all(send, 'dp', split_axis=0, concat_axis=0, tiled=True)  58.5 us
    reduce_scatter x1, waiting for transfers between devices, per_device(): summed = lax.psum_scatter(piece, 'expert', scatter_dimension=1, tiled=True)  38.4 us
    all_gather x1, waiting for transfers between devices, per_device(): blocks = lax.all_gather(part_2, 'expert')  31.5 us
    all_gather x1, waiting for transfers between devices, per_device(): inputs = lax.all_gather(got[:, :part], 'expert', axis=1, tiled=True)  30.4 us
    all_to_all x1, waiting for transfers between devices, per_device(): lax.all_to_all(jnp.concatenate([summed, tail], axis=1), 'dp', split_axis=...  15.6 us
    dot_general x4, matrix products, contract_first(): lax.dot_general(left, right, (((0,), (0,)), ((), ())), preferred_element_...  15.1 us
    dot_general x3, matrix products, contract_last(): lax.dot_general(left, right, (((1,), (1,)), ((), ())), preferred_element_...  8.84 us
    reshape x1, local copies, waits for them, and re-layouts, per_device(): upward = jnp.concatenate(blocks, axis=1)  6.2 us
  transfers between devices with their start and end apart: 4, of which 4 were waited for; matrix products, arithmetic and copies ran while one was open for 8% of the time, Pallas kernels for 0%

profile of v1, /device:TPU:0, one launch (start us, length us, event | category | flops | bytes accessed | tf_op | source)
XLA Modules:
  0.0 253.8 jit_solution(10908962109142438467)
XLA Ops:
  7.2 0.0 copy-start
  7.2 0.0 all-gather.6.cloned.1.call-start
  7.2 0.9 copy.30
  8.2 0.1 eq.35
  8.3 0.2 convert_reduce_fusion.2
  8.5 0.1 reduce_sum.48
  8.6 0.1 copy.31
  8.7 0.7 multiply_add_fusion
  9.4 0.7 convert_element_type.79
  10.1 1.0 constant_dynamic-slice_fusion
  11.0 0.2 convert_reduce_fusion
  11.2 1.6 convolution_convert_fusion.3
  12.9 0.1 broadcast_in_dim.62
  13.0 0.2 pad_maximum_fusion
  13.2 58.5 %all_to_all.24 = bf16[8,64,2176]{2,1,0:T(8,128)(2,1)S(1)} all-to-all(bf16[8,64,2176]{2,1,0:T(8,128)(2,1)S(1)} %bitcast.43), channel_id=1, replica_groups=mesh['dp'=8,'expert'=4] {'dp'}, dimensions={0} | all-to-all | bytes 4456448 | tf_op jit(solution)/shard_map/all_to_all | solution.py:68
  71.7 0.0 copy-start.1
  71.7 1.4 copy-done.1
  73.0 1.6 fusion.25
  74.6 0.0 all-gather.6.cloned.1.call-update
  74.7 0.0 all-gather.4.cloned.1.call-start
  74.7 0.7 all-gather.4.cloned.1.call-update
  75.4 0.0 reduce-scatter.2.cloned.1.call-start
  75.5 1.0 convert_reduce_fusion.1
  76.5 31.5 %all-gather.6.cloned.1.call-done = bf16[2048,1024]{1,0:T(8,128)(2,1)} async-done(((bf16[512,1024]{1,0:T(8,128)(2,1)}), bf16[2048,1024]{1,0:T(8,128)(2,1)}) %all-gather.6.cloned.1.call-update) | async-done | bytes 4194320 | tf_op jit(solution)/shard_map/all_gather | solution.py:71
  108.0 6.2 %copy.32 = bf16[512,4,1024]{0,2,1:T(8,128)(2,1)} copy(bf16[512,4,1024]{2,0,1:T(8,128)(2,1)} %bitcast.47) | data formatting | bytes 8388608 | tf_op jit(solution)/shard_map/reshape | solution.py:72
  114.2 30.4 %all-gather.4.cloned.1.call-done = bf16[512,4096]{1,0:T(8,128)(2,1)} async-done(((bf16[512,1024]{1,0:T(8,128)(2,1)}), bf16[512,4096]{1,0:T(8,128)(2,1)}) %all-gather.4.cloned.1.call-update) | async-done | bytes 4194320 | tf_op jit(solution)/shard_map/all_gather | solution.py:69
  144.6 0.0 copy-done
  144.6 0.0 copy-start.4
  144.6 0.0 copy-start.8
  144.6 4.2 %fusion.5 = f32[512,384]{0,1:T(8,128)S(1)} fusion(bf16[512,4096]{1,0:T(8,128)(2,1)} %all-gather.4.cloned.1.call-done, bf16[1,384,4096]{2,1,0:T(8,128)(2,1)S(1)} %copy-done), kind=kOutput, calls=%fused_computation.9 | convolution fusion | flops 1610612736 | bytes 8126464 | tf_op jit(solution)/shard_map/dot_general | solution.py:13
  148.7 0.0 copy-done.4
  148.8 0.2 copy-done.8
  149.0 0.0 copy-start.2
  149.0 0.0 copy-start.10
  149.0 1.8 fusion.8
  150.8 0.4 copy-done.2
  151.2 1.0 copy-done.10
  152.2 2.9 %fusion.13 = (f32[512]{0:T(512)S(1)}, bf16[512,384]{0,1:T(8,128)(2,1)}, bf16[512,384]{0,1:T(8,128)(2,1)S(1)}, bf16[512,384]{0,1:T(8,128)(2,1)S(1)}) fusion(f32[512,384]{0,1:T(8,128)S(1)} %fusion.8, f32[512,384]{0,1:T(8,128)S(1)} %fusion.5, f32[512]{0:T(512)S(1)} %convert_reduce_fusion.1, bf16[512,4096]{0,1:T(8,128)(2,1)S(1)} %bitcast.45, ...), kind=kOutput, calls=%fused_computation.23 | convolution fusion | flops 1614347776 | bytes 10096640 | tf_op jit(solution)/shard_map/dot_general | solution.py:13
  155.0 0.0 copy-start.7
  155.0 0.0 copy-start.5
  155.0 2.4 fusion.3
  157.4 0.0 copy-done.7
  157.4 0.0 copy-done.5
  157.5 4.6 %add_convert_fusion = bf16[512,4096]{1,0:T(8,128)(2,1)} fusion(f32[512,4096]{1,0:T(8,128)S(1)} %fusion.3, bf16[512,384]{0,1:T(8,128)(2,1)S(1)} %get-tuple-element.14, bf16[1,384,4096]{2,1,0:T(8,128)(2,1)S(1)} %copy-done.4), kind=kOutput, calls=%fused_computation | convolution fusion | flops 1614807040 | bytes 16121856 | tf_op jit(solution)/shard_map/dot_general | solution.py:40
  162.0 0.0 reduce-scatter.2.cloned.1.call-update
  162.1 5.9 %psum.7 = f32[512]{0:T(512)S(1)} all-reduce(f32[512]{0:T(512)S(1)} %get-tuple-element.9), channel_id=1, replica_groups=mesh['dp'=8,'expert'=4] {'expert'}, use_global_device_ids=true, to_apply=%region_5.6 | all-reduce | flops 512 | bytes 4096 | tf_op jit(solution)/shard_map/psum | solution.py:77
  168.0 0.2 broadcast_select_fusion
  168.2 38.4 %reduce-scatter.2.cloned.1.call-done = bf16[512,1024]{1,0:T(8,128)(2,1)} async-done(((bf16[512,4096]{1,0:T(8,128)(2,1)}), bf16[512,1024]{1,0:T(8,128)(2,1)}) %reduce-scatter.2.cloned.1.call-update) | async-done | bytes 1048592 | tf_op jit(solution)/shard_map/reduce_scatter | solution.py:78
  206.6 2.4 pad_maximum_fusion.1
  209.1 5.5 %all-to-all-start.1 = ((bf16[8,64,1152]{2,1,0:T(8,128)(2,1)}), bf16[8,64,1152]{2,1,0:T(8,128)(2,1)}, u32[]{:S(2)}, u32[]{:S(2)}) async-start(bf16[8,64,1152]{2,1,0:T(8,128)(2,1)} %bitcast.44), calls=%async_computation.2 | async-start | bytes 2359296 | tf_op jit(solution)/shard_map/all_to_all | solution.py:83
  214.6 0.0 copy-start.6
  214.6 0.0 copy-start.9
  214.6 5.9 %fusion = bf16[1,384,4096]{2,1,0:T(8,128)(2,1)} fusion(bf16[512,384]{0,1:T(8,128)(2,1)} %copy-done.7, bf16[512,4096]{1,0:T(8,128)(2,1)} %all-gather.4.cloned.1.call-done), kind=kOutput, calls=%fused_computation.4 | convolution fusion | flops 1612185600 | bytes 7733248 | tf_op jit(solution)/shard_map/dot_general | solution.py:19
  220.5 0.0 copy-done.6
  220.5 0.0 copy-done.9
  220.5 0.0 copy-start.11
  220.5 3.5 %fusion.1 = bf16[1,384,4096]{2,1,0:T(8,128)(2,1)} fusion(bf16[512,384]{0,1:T(8,128)(2,1)S(1)} %copy-done.6, bf16[512,4096]{1,0:T(8,128)(2,1)S(1)} %copy-done.9), kind=kOutput, calls=%fused_computation.5 | convolution fusion | flops 1612185600 | bytes 7733248 | tf_op jit(solution)/shard_map/dot_general | solution.py:19
  224.0 0.0 copy-done.3
  224.0 0.0 copy-done.11
  224.0 3.5 %fusion.2 = bf16[1,384,4096]{2,1,0:T(8,128)(2,1)} fusion(bf16[512,4096]{0,1:T(8,128)(2,1)S(1)} %bitcast.46, bf16[512,384]{0,1:T(8,128)(2,1)S(1)} %copy-done.11, f32[512]{0:T(512)S(1)} %convert_reduce_fusion.1), kind=kOutput, calls=%fused_computation.6 | convolution fusion | flops 1612775424 | bytes 7735296 | tf_op jit(solution)/shard_map/dot_general | solution.py:19
  227.5 15.6 %all-to-all-done.1 = bf16[8,64,1152]{2,1,0:T(8,128)(2,1)} async-done(((bf16[8,64,1152]{2,1,0:T(8,128)(2,1)}), bf16[8,64,1152]{2,1,0:T(8,128)(2,1)}, u32[]{:S(2)}, u32[]{:S(2)}) %all-to-all-start.1) | async-done | bytes 1179680 | tf_op jit(solution)/shard_map/all_to_all | solution.py:83
  243.1 2.3 convolution_convert_fusion.4
  245.4 1.2 add_reduce_fusion
  246.6 0.7 select_reduce_fusion
  (3 shorter events, 0.0 us)
Async XLA Ops:
  7.2 137.4 %copy-start = (bf16[1,384,4096]{2,1,0:T(8,128)(2,1)S(1)}, bf16[1,384,4096]{2,1,0:T(8,128)(2,1)}, u32[]{:S(2)}) copy-start(bf16[1,384,4096]{2,1,0:T(8,128)(2,1)} %param.11) | copy-start | bytes 9437188
  7.2 100.8 %all-gather.6.cloned.1.call-start = ((), (), s32[]{:S(2)}) async-start(), calls=%async_computation.5 | async-start | bytes 5242880 | tf_op jit(solution)/shard_map/all_gather | solution.py:71
  71.7 1.4 copy-start.1
  74.7 69.9 %all-gather.4.cloned.1.call-start = ((), (), s32[]{:S(2)}) async-start(), calls=%async_computation.3 | async-start | bytes 5242880 | tf_op jit(solution)/shard_map/all_gather | solution.py:69
  75.4 131.2 %reduce-scatter.2.cloned.1.call-start = ((), (), s32[]{:S(2)}) async-start(), calls=%async_computation.4 | async-start | bytes 5242880 | tf_op jit(solution)/shard_map/reduce_scatter | solution.py:78
  144.6 4.2 %copy-start.4 = (bf16[1,384,4096]{2,1,0:T(8,128)(2,1)S(1)}, bf16[1,384,4096]{2,1,0:T(8,128)(2,1)}, u32[]{:S(2)}) copy-start(bf16[1,384,4096]{2,1,0:T(8,128)(2,1)} %param.12) | copy-start | bytes 9437188
  144.6 4.4 %copy-start.8 = (bf16[512,4096]{1,0:T(8,128)(2,1)S(1)}, bf16[512,4096]{1,0:T(8,128)(2,1)}, u32[]{:S(2)}) copy-start(bf16[512,4096]{1,0:T(8,128)(2,1)} %all-gather.4.cloned.1.call-done) | copy-start | bytes 12582916
  149.0 2.2 copy-start.2
  149.0 3.2 %copy-start.10 = (bf16[1,384,4096]{2,1,0:T(8,128)(2,1)S(1)}, bf16[1,384,4096]{2,1,0:T(8,128)(2,1)}, u32[]{:S(2)}) copy-start(bf16[1,384,4096]{2,1,0:T(8,128)(2,1)} %param.13) | copy-start | bytes 9437188
  155.0 2.4 copy-start.7
  155.0 2.4 copy-start.5
  209.1 34.0 %all-to-all-start.1 = ((bf16[8,64,1152]{2,1,0:T(8,128)(2,1)}), bf16[8,64,1152]{2,1,0:T(8,128)(2,1)}, u32[]{:S(2)}, u32[]{:S(2)}) async-start(bf16[8,64,1152]{2,1,0:T(8,128)(2,1)} %bitcast.44), calls=%async_computation.2 | async-start | bytes 2359296 | tf_op jit(solution)/shard_map/all_to_all | solution.py:83
  214.6 5.9 %copy-start.6 = (bf16[512,384]{0,1:T(8,128)(2,1)S(1)}, bf16[512,384]{0,1:T(8,128)(2,1)}, u32[]{:S(2)}) copy-start(bf16[512,384]{0,1:T(8,128)(2,1)} %copy-done.5) | copy-start | bytes 1179652
  214.6 5.9 %copy-start.9 = (bf16[512,4096]{1,0:T(8,128)(2,1)S(1)}, bf16[512,4096]{1,0:T(8,128)(2,1)}, u32[]{:S(2)}) copy-start(bf16[512,4096]{1,0:T(8,128)(2,1)} %all-gather.4.cloned.1.call-done) | copy-start | bytes 12582916
  220.5 3.5 %copy-start.3 = (bf16[512,4,1024]{0,2,1:T(8,128)(2,1)S(1)}, bf16[512,4,1024]{0,2,1:T(8,128)(2,1)}, u32[]{:S(2)}) copy-start(bf16[512,4,1024]{0,2,1:T(8,128)(2,1)} %copy.32) | copy-start | bytes 12582916
  220.5 3.5 %copy-start.11 = (bf16[512,384]{0,1:T(8,128)(2,1)S(1)}, bf16[512,384]{0,1:T(8,128)(2,1)}, u32[]{:S(2)}) copy-start(bf16[512,384]{0,1:T(8,128)(2,1)} %get-tuple-element.10) | copy-start | bytes 1179652
Sparse Core Ops, SparseCore 0:
  74.8 33.1 all-gather.5
  110.1 34.4 all-gather.3
  162.2 44.3 reduce-scatter.1
